TPU v7x, 256 devices: a whole 4x4x8 slice. The times are simulated.
256 devices in a mesh: task: 8 (over z_hi, core), row: 8 (over x, z_lo), col: 4 (over y).
Axes of the slice: x: 4, y: 4, z: 8 (z_hi: 4, z_lo: 2; z = z_hi * 2 + z_lo), core: 2. Of those that a mesh axis runs over, the one named last changes fastest.
Arguments:
- activations: bfloat16 [8, 512, 13824], P('task', 'col', 'row'), may hold values from -6 to 6
- weights: bfloat16 [8, 13824, 5120], P('task', 'row', 'col'), may hold values from -0.0625 to 0.0625
- labels: int32 [8, 512], P('task'), may hold values from 0 to 127
- prototypes: bfloat16 [8, 128, 5120], P('task', None, 'col'), may hold values from -6 to 6
Outputs:
- merged: bfloat16 [13824, 5120], P('row', 'col')
- merged_out: bfloat16 [8, 512, 5120], P('task', 'row', 'col')
All inputs are finite; a program needn't handle non-finite values.
Results may differ from a plain program's by a relative error of at most 0.02.
Values may be sent and summed in bfloat16 or wider, within the bound.
A program may use at most 128 MiB of HBM per device.

v0:
```python
import jax
import jax.numpy as jnp
from jax import lax
from jax.sharding import PartitionSpec as P


def class_targets(label_rows, protos):
    count = label_rows.shape[0]
    onehot = (
        label_rows[:, None] == lax.broadcasted_iota(jnp.int32, (count, protos.shape[0]), 1)
    ).astype(jnp.bfloat16)
    return jnp.dot(onehot, protos, preferred_element_type=jnp.float32)


def local(activations, weights, labels, prototypes):
    acts = activations[0]
    weight = weights[0]
    label_row = labels[0]
    protos = prototypes[0]
    full_acts = lax.all_gather(acts, "col", axis=0, tiled=True)
    partial_out = jnp.dot(full_acts, weight, preferred_element_type=jnp.float32)
    output = lax.psum(partial_out.astype(jnp.bfloat16), "row").astype(jnp.float32)
    grad = output - class_targets(label_row, protos)
    gsq = (grad * grad).astype(jnp.bfloat16)
    wide = full_acts.astype(jnp.float32)
    asq = (wide * wide).astype(jnp.bfloat16)
    fisher = lax.dot_general(asq, gsq, (((0,), (0,)), ((), ())), preferred_element_type=jnp.float32)
    weighted = fisher * weight.astype(jnp.float32)
    numer, denom = (
        lax.psum_scatter(weighted, "task", scatter_dimension=0, tiled=True),
        lax.psum_scatter(fisher, "task", scatter_dimension=0, tiled=True),
    )
    piece = (numer / (denom + 1e-06)).astype(jnp.bfloat16)
    merged = lax.all_gather(piece, "task", axis=0, tiled=True)
    result = lax.psum_scatter(
        jnp.dot(full_acts, merged, preferred_element_type=jnp.float32).astype(jnp.bfloat16),
        "row",
        scatter_dimension=0,
        tiled=True,
    )
    return (merged, result[None])


def solution(mesh):
    placed = (
        P("task", "col", "row"),
        P("task", "row", "col"),
        P("task", None),
        P("task", None, "col"),
    )
    return jax.shard_map(
        local,
        mesh=mesh,
        in_specs=placed,
        out_specs=(P("row", "col"), P("task", "row", "col")),
        check_vma=False,
    )
```

profile of v0, /device:TPU:8, one launch (start us, length us, event | category | flops | bytes accessed | tf_op | source)
XLA Modules:
  0.0 475.8 jit_solution(1805810077636972893)
XLA Ops:
  7.2 0.0 all-gather.6.cloned.1.call-start
  7.2 0.7 all-gather.6.cloned.1.call-update
  7.9 0.0 all-reduce.2.cloned.1.call-start
  8.0 38.4 %all-gather.6.cloned.1.call-done = bf16[1,512,1728]{1,2,0:T(8,128)(2,1)} async-done(((bf16[1,128,1728]{1,2,0:T(8,128)(2,1)}), bf16[1,512,1728]{1,2,0:T(8,128)(2,1)}) %all-gather.6.cloned.1.call-update) | async-done | bytes 1769488 | tf_op jit(solution)/shard_map/all_gather | solution.py:20
  46.4 6.6 %fusion.4 = bf16[512,1280]{1,0:T(8,128)(2,1)} fusion(bf16[1,1728,1280]{2,1,0:T(8,128)(2,1)} %param.5, bf16[1,512,1728]{1,2,0:T(8,128)(2,1)} %all-gather.6.cloned.1.call-done), kind=kOutput, calls=%fused_computation.7 | convolution fusion | flops 2265579520 | bytes 7503872 | tf_op jit(solution)/shard_map/dot_general | solution.py:21
  53.0 0.0 all-reduce.2.cloned.1.call-update
  53.0 0.0 reduce-scatter.6.cloned.1.call-start
  53.1 90.5 %all-reduce.2.cloned.1.call-done = bf16[512,1280]{1,0:T(8,128)(2,1)} async-done(((bf16[512,1280]{1,0:T(8,128)(2,1)}), bf16[512,1280]{1,0:T(8,128)(2,1)}) %all-reduce.2.cloned.1.call-update) | async-done | bytes 1310736 | tf_op jit(solution)/shard_map/psum | solution.py:22
  143.6 9.8 %convert_multiply_fusion = (f32[1728,1280]{1,0:T(8,128)}, f32[1728,1280]{1,0:T(8,128)}) fusion(bf16[1,1728,1280]{2,1,0:T(8,128)(2,1)} %param.5, bf16[512,1280]{1,0:T(8,128)(2,1)} %all-reduce.2.cloned.1.call-done, bf16[1,128,1280]{2,1,0:T(8,128)(2,1)S(1)} %copy-done, s32[512]{0:T(512)S(1)} %bitcast.30, bf16[1,512,1728]{1,2,0:T(8,128)(2,1)S(1)} %copy-done.1), kind=kOutput, calls=%fused_computation | convolution fusion | flops 2442461184 | bytes 25528320 | tf_op jit(solution)/shard_map/dot_general | solution.py:27
  153.4 0.0 reduce-scatter.6.cloned.1.call-update
  153.4 0.0 reduce-scatter.8.cloned.1.call-start
  153.4 0.5 reduce-scatter.8.cloned.1.call-update
  154.0 0.0 all-gather.4.cloned.1.call-start
  154.0 96.8 %reduce-scatter.6.cloned.1.call-done = f32[216,1280]{1,0:T(8,128)} async-done(((f32[1728,1280]{1,0:T(8,128)}), f32[216,1280]{1,0:T(8,128)}) %reduce-scatter.6.cloned.1.call-update) | async-done | bytes 1105936 | tf_op jit(solution)/shard_map/reduce_scatter | solution.py:30
  250.8 104.8 %reduce-scatter.8.cloned.1.call-done = f32[216,1280]{1,0:T(8,128)} async-done(((f32[1728,1280]{1,0:T(8,128)}), f32[216,1280]{1,0:T(8,128)}) %reduce-scatter.8.cloned.1.call-update) | async-done | bytes 1105936 | tf_op jit(solution)/shard_map/reduce_scatter | solution.py:31
  355.7 2.5 divide_convert_fusion
  358.2 0.0 reduce-scatter.10.cloned.1.call-start
  358.3 54.9 %all-gather.4.cloned.1.call-done = bf16[1728,1280]{1,0:T(8,128)(2,1)} async-done(((bf16[216,1280]{1,0:T(8,128)(2,1)}), bf16[1728,1280]{1,0:T(8,128)(2,1)}) %all-gather.4.cloned.1.call-update) | async-done | bytes 4423696 | tf_op jit(solution)/shard_map/all_gather | solution.py:34
  413.1 4.8 %fusion.7 = bf16[512,1280]{0,1:T(8,128)(2,1)S(1)} fusion(bf16[1728,1280]{1,0:T(8,128)(2,1)} %all-gather.4.cloned.1.call-done, bf16[1,512,1728]{1,2,0:T(8,128)(2,1)S(1)} %copy-done.1), kind=kOutput, calls=%fused_computation.9 | convolution fusion | flops 2265579520 | bytes 7503872 | tf_op jit(solution)/shard_map/dot_general | solution.py:36
  418.0 1.4 copy.8
  419.4 42.9 %reduce-scatter.10.cloned.1.call-done = bf16[64,1280]{1,0:T(8,128)(2,1)} async-done(((bf16[512,1280]{1,0:T(8,128)(2,1)}), bf16[64,1280]{1,0:T(8,128)(2,1)}) %reduce-scatter.10.cloned.1.call-update) | async-done | bytes 163856
  462.4 1.1 copy.9
  463.5 0.8 copy.7
  464.3 4.6 copy.12
  (8 shorter events, 0.0 us)
Async XLA Ops:
  7.2 136.4 %copy-start = (bf16[1,128,1280]{2,1,0:T(8,128)(2,1)S(1)}, bf16[1,128,1280]{2,1,0:T(8,128)(2,1)}, u32[]{:S(2)}) copy-start(bf16[1,128,1280]{2,1,0:T(8,128)(2,1)} %param.7) | copy-start | bytes 983044
  7.2 39.2 %all-gather.6.cloned.1.call-start = ((), (), s32[]{:S(2)}) async-start(), calls=%async_computation.7 | async-start | bytes 2211840 | tf_op jit(solution)/shard_map/all_gather | solution.py:20
  7.9 135.7 %copy-start.2 = (s32[1,512]{1,0:T(1,128)S(1)}, s32[1,512]{1,0:T(1,128)}, u32[]{:S(2)}) copy-start(s32[1,512]{1,0:T(1,128)} %param.6) | copy-start | bytes 6148
  7.9 135.7 %all-reduce.2.cloned.1.call-start = ((), (), s32[]{:S(2)}) async-start(), calls=%async_computation.3 | async-start | bytes 2621440 | tf_op jit(solution)/shard_map/psum | solution.py:22
  46.4 97.2 %copy-start.1 = (bf16[1,512,1728]{1,2,0:T(8,128)(2,1)S(1)}, bf16[1,512,1728]{1,2,0:T(8,128)(2,1)}, u32[]{:S(2)}) copy-start(bf16[1,512,1728]{1,2,0:T(8,128)(2,1)} %all-gather.6.cloned.1.call-done) | copy-start | bytes 5308420
  53.0 197.8 %reduce-scatter.6.cloned.1.call-start = ((), (), s32[]{:S(2)}) async-start(), calls=%async_computation.4 | async-start | bytes 9953280 | tf_op jit(solution)/shard_map/reduce_scatter | solution.py:30
  153.4 202.3 %reduce-scatter.8.cloned.1.call-start = ((), (), s32[]{:S(2)}) async-start(), calls=%async_computation.5 | async-start | bytes 9953280 | tf_op jit(solution)/shard_map/reduce_scatter | solution.py:31
  154.0 259.2 %all-gather.4.cloned.1.call-start = ((), (), s32[]{:S(2)}) async-start(), calls=%async_computation.6 | async-start | bytes 4976640 | tf_op jit(solution)/shard_map/all_gather | solution.py:34
  358.2 104.1 %reduce-scatter.10.cloned.1.call-start = ((), (), s32[]{:S(2)}) async-start(), calls=%async_computation.8 | async-start | bytes 1474560
Sparse Core Ops, SparseCore 0:
  9.8 36.5 all-gather.5
  53.1 90.4 all-reduce.1
  153.5 97.2 reduce-scatter.5
  253.4 102.1 reduce-scatter.7
  358.3 54.7 all-gather.3
  419.6 42.7 reduce-scatter.9
where the time goes:
time: 476 us
  waiting for transfers between devices  430 us (90%)
  matrix products  21.2 us (4%)
  between operations  14.1 us (3%)
  local copies, waits for them, and re-layouts  8.06 us (2%)
    reduce_scatter x1, waiting for transfers between devices, local(): lax.psum_scatter(fisher, 'task', scatter_dimension=0, tiled=True)  105 us
    reduce_scatter x1, waiting for transfers between devices, local(): lax.psum_scatter(weighted, 'task', scatter_dimension=0, tiled=True)  96.8 us
    psum x1, waiting for transfers between devices, local(): lax.psum(partial_out.astype(jnp.bfloat16), 'row').astype(jnp.float32)  90.5 us
    all_gather x1, waiting for transfers between devices, local(): merged = lax.all_gather(piece, 'task', axis=0, tiled=True)  54.9 us
    unnamed x7, waiting for transfers between devices  44.2 us
    all_gather x1, waiting for transfers between devices, local(): full_acts = lax.all_gather(acts, 'col', axis=0, tiled=True)  38.4 us
    dot_general x1, matrix products, local(): lax.dot_general(asq, gsq, (((0,), (0,)), ((), ())), preferred_element_typ...  9.77 us
  transfers between devices with their start and end apart: 6, of which 6 were waited for; matrix products, arithmetic and copies ran while one was open for 0% of the time, Pallas kernels for 0%

commit v1 on v0

--- a/solution.py
+++ b/solution.py
@@ -2,6 +2,11 @@
 import jax.numpy as jnp
 from jax import lax
 from jax.sharding import PartitionSpec as P
+
+
+def exchange_gather(shard, axis, dim):
+    stack = jnp.stack([shard] * lax.axis_size(axis))
+    return jnp.concatenate(lax.all_to_all(stack, axis, 0, 0), axis=dim)
 
 
 def class_targets(label_rows, protos):
@@ -31,7 +36,7 @@
         lax.psum_scatter(fisher, "task", scatter_dimension=0, tiled=True),
     )
     piece = (numer / (denom + 1e-06)).astype(jnp.bfloat16)
-    merged = lax.all_gather(piece, "task", axis=0, tiled=True)
+    merged = exchange_gather(piece, "task", 0)
     result = lax.psum_scatter(
         jnp.dot(full_acts, merged, preferred_element_type=jnp.float32).astype(jnp.bfloat16),
         "row",

time: 476 us -> 525 us (1.10)
  blocking collectives: 0 us -> 107 us
  waiting for transfers between devices: 430 us -> 373 us
    all_to_all x0 -> x1, blocking collectives: none -> 107 us  [exchange_gather(): return jnp.concatenate(lax.all_to_all(stack, axis, 0, 0), axis=dim)]
    all_gather x1 -> x0, waiting for transfers between devices: 54.9 us -> none  [local(): merged = lax.all_gather(piece, 'task', axis=0, tiled=True)]
    unnamed x7 -> x6, waiting for transfers between devices: 44.2 us -> 42.4 us
  transfers between devices with their start and end apart: 6 -> 5, of which waited for: 6 -> 5; matrix products, arithmetic and copies ran while one was open for 0% -> 0% of each run, Pallas kernels for 0% -> 0%
where the time goes in v1:
time: 525 us
  waiting for transfers between devices  373 us (71%)
  blocking collectives  107 us (20%)
  matrix products  19 us (4%)
  between operations  13.8 us (3%)
  local copies, waits for them, and re-layouts  10.3 us (2%)
    all_to_all x1, blocking collectives, exchange_gather(): return jnp.concatenate(lax.all_to_all(stack, axis, 0, 0), axis=dim)  107 us
    reduce_scatter x1, waiting for transfers between devices, local(): lax.psum_scatter(fisher, 'task', scatter_dimension=0, tiled=True)  105 us
    reduce_scatter x1, waiting for transfers between devices, local(): lax.psum_scatter(weighted, 'task', scatter_dimension=0, tiled=True)  96.8 us
    psum x1, waiting for transfers between devices, local(): lax.psum(partial_out.astype(jnp.bfloat16), 'row').astype(jnp.float32)  90.5 us
    unnamed x6, waiting for transfers between devices  42.4 us
    all_gather x1, waiting for transfers between devices, local(): full_acts = lax.all_gather(acts, 'col', axis=0, tiled=True)  38.4 us
  transfers between devices with their start and end apart: 5, of which 5 were waited for; matrix products, arithmetic and copies ran while one was open for 0% of the time, Pallas kernels for 0%

profile of v1, /device:TPU:8, one launch (start us, length us, event | category | flops | bytes accessed | tf_op | source)
XLA Modules:
  0.0 524.7 jit_solution(12576227571012848471)
XLA Ops:
  7.2 0.0 all-gather.3.cloned.1.call-start
  7.2 0.7 all-gather.3.cloned.1.call-update
  7.9 0.0 all-reduce.2.cloned.1.call-start
  8.0 38.4 %all-gather.3.cloned.1.call-done = bf16[1,512,1728]{1,2,0:T(8,128)(2,1)} async-done(((bf16[1,128,1728]{1,2,0:T(8,128)(2,1)}), bf16[1,512,1728]{1,2,0:T(8,128)(2,1)}) %all-gather.3.cloned.1.call-update) | async-done | bytes 1769488 | tf_op jit(solution)/shard_map/all_gather | solution.py:25
  46.4 6.6 %fusion.4 = bf16[512,1280]{1,0:T(8,128)(2,1)} fusion(bf16[1,1728,1280]{2,1,0:T(8,128)(2,1)} %param.5, bf16[1,512,1728]{1,2,0:T(8,128)(2,1)} %all-gather.3.cloned.1.call-done), kind=kOutput, calls=%fused_computation.7 | convolution fusion | flops 2265579520 | bytes 7503872 | tf_op jit(solution)/shard_map/dot_general | solution.py:26
  53.0 0.0 all-reduce.2.cloned.1.call-update
  53.0 0.0 reduce-scatter.6.cloned.1.call-start
  53.1 90.5 %all-reduce.2.cloned.1.call-done = bf16[512,1280]{1,0:T(8,128)(2,1)} async-done(((bf16[512,1280]{1,0:T(8,128)(2,1)}), bf16[512,1280]{1,0:T(8,128)(2,1)}) %all-reduce.2.cloned.1.call-update) | async-done | bytes 1310736 | tf_op jit(solution)/shard_map/psum | solution.py:27
  143.6 9.8 %convert_multiply_fusion = (f32[1728,1280]{1,0:T(8,128)}, f32[1728,1280]{1,0:T(8,128)}) fusion(bf16[1,1728,1280]{2,1,0:T(8,128)(2,1)} %param.5, bf16[512,1280]{1,0:T(8,128)(2,1)} %all-reduce.2.cloned.1.call-done, bf16[1,128,1280]{2,1,0:T(8,128)(2,1)S(1)} %copy-done, s32[512]{0:T(512)S(1)} %bitcast.33, bf16[1,512,1728]{1,2,0:T(8,128)(2,1)S(1)} %copy-done.2), kind=kOutput, calls=%fused_computation | convolution fusion | flops 2442461184 | bytes 25528320 | tf_op jit(solution)/shard_map/dot_general | solution.py:32
  153.4 0.0 reduce-scatter.8.cloned.1.call-start
  153.4 0.5 reduce-scatter.8.cloned.1.call-update
  154.0 0.0 reduce-scatter.10.cloned.1.call-start
  154.0 96.8 %reduce-scatter.6.cloned.1.call-done = f32[216,1280]{1,0:T(8,128)} async-done(((f32[1728,1280]{1,0:T(8,128)}), f32[216,1280]{1,0:T(8,128)}) %reduce-scatter.6.cloned.1.call-update) | async-done | bytes 1105936 | tf_op jit(solution)/shard_map/reduce_scatter | solution.py:35
  250.8 104.8 %reduce-scatter.8.cloned.1.call-done = f32[216,1280]{1,0:T(8,128)} async-done(((f32[1728,1280]{1,0:T(8,128)}), f32[216,1280]{1,0:T(8,128)}) %reduce-scatter.8.cloned.1.call-update) | async-done | bytes 1105936 | tf_op jit(solution)/shard_map/reduce_scatter | solution.py:36
  355.7 1.7 divide_convert_fusion
  357.4 0.3 stack.2
  357.7 106.7 %all_to_all.5 = bf16[8,216,1280]{2,1,0:T(8,128)(2,1)S(1)} all-to-all(bf16[8,216,1280]{2,1,0:T(8,128)(2,1)S(1)} %stack.2), channel_id=1, replica_groups=mesh['task'=8,'row'=8,'col'=4] {'task'}, dimensions={0} | all-to-all | bytes 8847360 | tf_op jit(solution)/shard_map/all_to_all | solution.py:9
  464.4 2.0 copy-done.1
  466.4 2.6 fusion.7
  469.0 1.4 copy.8
  470.5 41.1 %reduce-scatter.10.cloned.1.call-done = bf16[64,1280]{1,0:T(8,128)(2,1)} async-done(((bf16[512,1280]{1,0:T(8,128)(2,1)}), bf16[64,1280]{1,0:T(8,128)(2,1)}) %reduce-scatter.10.cloned.1.call-update) | async-done | bytes 163856
  511.6 1.1 copy.9
  512.7 0.8 copy.7
  513.5 4.6 copy.12
  (9 shorter events, 0.1 us)
Async XLA Ops:
  7.2 136.4 %copy-start = (bf16[1,128,1280]{2,1,0:T(8,128)(2,1)S(1)}, bf16[1,128,1280]{2,1,0:T(8,128)(2,1)}, u32[]{:S(2)}) copy-start(bf16[1,128,1280]{2,1,0:T(8,128)(2,1)} %param.7) | copy-start | bytes 983044
  7.2 39.2 %all-gather.3.cloned.1.call-start = ((), (), s32[]{:S(2)}) async-start(), calls=%async_computation.7 | async-start | bytes 2211840 | tf_op jit(solution)/shard_map/all_gather | solution.py:25
  7.9 135.7 %copy-start.3 = (s32[1,512]{1,0:T(1,128)S(1)}, s32[1,512]{1,0:T(1,128)}, u32[]{:S(2)}) copy-start(s32[1,512]{1,0:T(1,128)} %param.6) | copy-start | bytes 6148
  7.9 135.7 %all-reduce.2.cloned.1.call-start = ((), (), s32[]{:S(2)}) async-start(), calls=%async_computation.4 | async-start | bytes 2621440 | tf_op jit(solution)/shard_map/psum | solution.py:27
  46.4 97.2 %copy-start.2 = (bf16[1,512,1728]{1,2,0:T(8,128)(2,1)S(1)}, bf16[1,512,1728]{1,2,0:T(8,128)(2,1)}, u32[]{:S(2)}) copy-start(bf16[1,512,1728]{1,2,0:T(8,128)(2,1)} %all-gather.3.cloned.1.call-done) | copy-start | bytes 5308420
  53.0 197.8 %reduce-scatter.6.cloned.1.call-start = ((), (), s32[]{:S(2)}) async-start(), calls=%async_computation.5 | async-start | bytes 9953280 | tf_op jit(solution)/shard_map/reduce_scatter | solution.py:35
  153.4 202.3 %reduce-scatter.8.cloned.1.call-start = ((), (), s32[]{:S(2)}) async-start(), calls=%async_computation.6 | async-start | bytes 9953280 | tf_op jit(solution)/shard_map/reduce_scatter | solution.py:36
  154.0 357.6 %reduce-scatter.10.cloned.1.call-start = ((), (), s32[]{:S(2)}) async-start(), calls=%async_computation.8 | async-start | bytes 1474560
  464.4 2.0 copy-start.1
Sparse Core Ops, SparseCore 0:
  9.8 36.5 all-gather.2
  53.1 90.4 all-reduce.1
  153.5 97.2 reduce-scatter.5
  253.5 102.1 reduce-scatter.7
  470.6 40.9 reduce-scatter.9
